TPU v7x, 256 devices: a whole 4x4x8 slice. The times are simulated.
256 devices in a mesh: dp: 32 (over y, x, core), tsp: 8 (over z).
Axes of the slice: x: 4, y: 4, z: 8, core: 2. Of those that a mesh axis runs over, the one named last changes fastest.
Arguments:
- tokens: bfloat16 [65536, 8192], P('dp', 'tsp'), may hold values from -6 to 6
- cotangent: bfloat16 [65536, 1024], P('dp', 'tsp'), may hold values from -6 to 6
- frozen_key_weight: bfloat16 [8192, 1024], P('tsp'), may hold values from -0.1875 to 0.1875
- adapter_down_weight: bfloat16 [64, 64, 8192], P('dp', None, 'tsp'), may hold values from -0.0625 to 0.0625
- adapter_up_weight: bfloat16 [64, 64, 1024], P('dp', None, 'tsp'), may hold values from -0.1875 to 0.1875
- adapter_place_table: int32 [64], replicated, may hold values from 0 to 63, as said below
- segment_adapter: int32 [512], P('dp'), may hold values from 0 to 63, as said below
- segment_live_count: int32 [512], P('dp'), may hold values from 1 to 128, as said below
Outputs:
- token_gradient: bfloat16 [65536, 8192], P('dp', 'tsp')
- down_grad: float32 [64, 64, 8192], P('dp', None, 'tsp')
- up_grad: float32 [64, 64, 1024], P('dp', None, 'tsp')
Inputs may be any that keep to these rules, and one draw needn't show every extreme that they name: A permutation: adapter a is held at place adapter_place_table[a], that is by the dp index adapter_place_table[a] // 2 as its entry adapter_place_table[a] % 2; the adapters' arrays and gradients are indexed by place. `segment_adapter`: the 16 segments of one dp index name at most one adapter held by any one dp index; an adapter may be named by several of them. `segment_live_count`: the live rows stand at the start of each segment; on every dp index some segment is full.
All inputs are finite; a program needn't handle non-finite values.
Results may differ from a plain program's by a relative error of at most 0.0034.
Values may be sent and summed in bfloat16 or wider, within the bound.
A program may use at most 128 MiB of HBM per device.

v0:
```python
import jax
import jax.numpy as jnp
from jax import lax
from jax.sharding import PartitionSpec as P

ADAPTER_SCALE = 2.0


def lookup(idents, mapping):
    matches = idents[:, None] == jnp.arange(mapping.shape[0], dtype=jnp.int32)[None, :]
    return jnp.sum(jnp.where(matches, mapping[None, :], 0), axis=1)


def on_device(
    tokens,
    cotangent,
    frozen_key_weight,
    adapter_down_weight,
    adapter_up_weight,
    adapter_place_table,
    segment_adapter,
    segment_live_count,
):
    dp_count = lax.axis_size("dp")
    places_per_device = adapter_down_weight.shape[0]
    rank_of_adapter = adapter_down_weight.shape[1]
    width_per_device = tokens.shape[1]
    key_dev = cotangent.shape[1]
    segments_per_device = segment_adapter.shape[0]
    segment_token_rows = tokens.shape[0] // segments_per_device
    adapter_places = lookup(segment_adapter, adapter_place_table)
    seg_owner = adapter_places // places_per_device
    seg_entry = adapter_places % places_per_device
    owner_hit = seg_owner[:, None] == jnp.arange(dp_count, dtype=jnp.int32)[None, :]
    wanted = jnp.max(jnp.where(owner_hit, seg_entry[:, None], -1), axis=0)
    incoming = lax.all_to_all(wanted[:, None], "dp", split_axis=0, concat_axis=0, tiled=True)[:, 0]
    serving_mesh = (
        incoming[:, None] == jnp.arange(places_per_device, dtype=jnp.int32)[None, :]
    ).astype(jnp.bfloat16)
    reply_down = jnp.einsum(
        "ap,phc->ahc", serving_mesh, adapter_down_weight, preferred_element_type=jnp.float32
    ).astype(jnp.bfloat16)
    reply_up = jnp.einsum(
        "hv,vun->hun", serving_mesh, adapter_up_weight, preferred_element_type=jnp.float32
    ).astype(jnp.bfloat16)
    fetched_down, fetched_up = (
        lax.all_to_all(reply_down, "dp", split_axis=0, concat_axis=0, tiled=True),
        lax.all_to_all(reply_up, "dp", split_axis=0, concat_axis=0, tiled=True),
    )
    picker = owner_hit.astype(jnp.bfloat16)
    segment_down_weight = jnp.einsum(
        "go,ord->grd", picker, fetched_down, preferred_element_type=jnp.float32
    ).astype(jnp.bfloat16)
    segment_up_weight = jnp.einsum(
        "go,ork->grk", picker, fetched_up, preferred_element_type=jnp.float32
    ).astype(jnp.bfloat16)
    seg_tokens = tokens.reshape(segments_per_device, segment_token_rows, width_per_device)
    seg_cotangent = cotangent.reshape(segments_per_device, segment_token_rows, key_dev)
    live_rows = (
        jnp.arange(segment_token_rows, dtype=jnp.int32)[None, :] < segment_live_count[:, None]
    ).astype(jnp.float32)
    partial_terms = jnp.concatenate(
        [
            jnp.einsum(
                "gtd,grd->gtr", seg_tokens, segment_down_weight, preferred_element_type=jnp.float32
            ),
            jnp.einsum(
                "gtk,grk->gtr", seg_cotangent, segment_up_weight, preferred_element_type=jnp.float32
            ),
        ],
        axis=2,
    )
    summed = lax.psum(partial_terms, "tsp")
    reduced_rows = (summed[:, :, :rank_of_adapter] * live_rows[:, :, None]).astype(jnp.bfloat16)
    gathered_weights = (summed[:, :, rank_of_adapter:] * live_rows[:, :, None]).astype(jnp.bfloat16)
    frozen_output = lax.dot_general(
        lax.all_gather(cotangent, "tsp", axis=1, tiled=True),
        frozen_key_weight,
        (((1,), (1,)), ((), ())),
        preferred_element_type=jnp.float32,
    )
    adapter_output = jnp.einsum(
        "wks,wsx->wkx", gathered_weights, segment_down_weight, preferred_element_type=jnp.float32
    )
    token_gradient = (
        frozen_output.reshape(segments_per_device, segment_token_rows, width_per_device)
        + ADAPTER_SCALE * adapter_output
    ) * live_rows[:, :, None]
    token_gradient = token_gradient.reshape(
        segments_per_device * segment_token_rows, width_per_device
    ).astype(jnp.bfloat16)
    gradient_scale = ADAPTER_SCALE / segment_token_rows
    segment_down_gradient = jnp.einsum(
        "upf,upb->ufb", gathered_weights, seg_tokens, preferred_element_type=jnp.float32
    )
    segment_up_gradient = jnp.einsum(
        "ija,ijn->ian", reduced_rows, seg_cotangent, preferred_element_type=jnp.float32
    )
    picker_f = owner_hit.astype(jnp.float32)
    slot_dgrad = (
        jnp.einsum("go,grd->ord", picker_f, segment_down_gradient, precision=lax.Precision.HIGHEST)
        * gradient_scale
    )
    slot_ugrad = (
        jnp.einsum("go,grk->ork", picker_f, segment_up_gradient, precision=lax.Precision.HIGHEST)
        * gradient_scale
    )
    slot_match = (wanted[:, None] == jnp.arange(places_per_device, dtype=jnp.int32)[None, :])[
        :, :, None, None
    ]
    dense_down = jnp.where(slot_match, slot_dgrad[:, None], 0.0).reshape(
        dp_count * places_per_device, rank_of_adapter, width_per_device
    )
    dense_up = jnp.where(slot_match, slot_ugrad[:, None], 0.0).reshape(
        dp_count * places_per_device, rank_of_adapter, key_dev
    )
    down_grad, up_grad = (
        lax.psum_scatter(dense_down, "dp", scatter_dimension=0, tiled=True),
        lax.psum_scatter(dense_up, "dp", scatter_dimension=0, tiled=True),
    )
    return (token_gradient, down_grad, up_grad)


def solution(mesh):
    placed = (
        P("dp", "tsp"),
        P("dp", "tsp"),
        P("tsp", None),
        P("dp", None, "tsp"),
        P("dp", None, "tsp"),
        P(),
        P("dp"),
        P("dp"),
    )
    return jax.shard_map(
        on_device,
        mesh=mesh,
        in_specs=placed,
        out_specs=(P("dp", "tsp"), P("dp", None, "tsp"), P("dp", None, "tsp")),
        check_vma=False,
    )
```

profile of v0, /device:TPU:2, one launch (start us, length us, event | category | flops | bytes accessed | tf_op | source)
XLA Modules:
  0.0 471.3 jit_solution(15498572598505192805)
XLA Ops:
  7.2 0.0 copy-start
  7.2 1.0 select_reduce_fusion.1
  8.2 0.1 select_reduce_fusion
  8.3 0.1 copy.57
  8.4 13.6 %all_to_all.19 = s32[32,1,1]{2,1,0:T(1,128)S(1)} all-to-all(s32[32,1,1]{2,1,0:T(1,128)S(1)} %copy.57), channel_id=1, replica_groups=mesh['dp'=32,'tsp'=8] {'dp'}, dimensions={0} | all-to-all | bytes 256 | tf_op jit(solution)/shard_map/all_to_all | solution.py:36
  22.0 0.7 reduce
  22.6 1.1 convolution_convert_fusion.1
  23.8 1.0 copy.63
  24.8 5.0 %all-to-all-start.2 = ((bf16[32,64,128]{2,1,0:T(8,128)(2,1)}), bf16[32,64,128]{2,1,0:T(8,128)(2,1)S(1)}, u32[]{:S(2)}, u32[]{:S(2)}) async-start(bf16[32,64,128]{2,1,0:T(8,128)(2,1)} %copy.63), calls=%async_computation.2 | async-start | bytes 1048576 | tf_op jit(solution)/shard_map/all_to_all | solution.py:48
  29.8 2.3 convolution_convert_fusion
  32.0 4.3 copy.59
  36.4 0.0 copy-start.4
  36.4 3.9 all-to-all-done.2
  40.2 5.9 %all-to-all-start.1 = ((bf16[32,64,1024]{2,1,0:T(8,128)(2,1)}), bf16[32,64,1024]{2,1,0:T(8,128)(2,1)}, u32[]{:S(2)}, u32[]{:S(2)}) async-start(bf16[32,64,1024]{2,1,0:T(8,128)(2,1)} %copy.59), calls=%async_computation.1 | async-start | bytes 8388608 | tf_op jit(solution)/shard_map/all_to_all | solution.py:47
  46.2 0.2 all-reduce.2.cloned.1.call-start
  46.4 0.4 convolution_convert_fusion.2
  46.8 0.0 copy-done.4
  46.8 0.4 convolution_bitcast_fusion
  47.3 50.4 %all-to-all-done.1 = bf16[32,64,1024]{2,1,0:T(8,128)(2,1)} async-done(((bf16[32,64,1024]{2,1,0:T(8,128)(2,1)}), bf16[32,64,1024]{2,1,0:T(8,128)(2,1)}, u32[]{:S(2)}, u32[]{:S(2)}) %all-to-all-start.1) | async-done | bytes 4194336 | tf_op jit(solution)/shard_map/all_to_all | solution.py:47
  97.7 0.0 copy-start.3
  97.7 6.9 %fusion.6 = bf16[16,64,1024]{2,0,1:T(8,128)(2,1)S(1)} fusion(bf16[32,64,1024]{2,1,0:T(8,128)(2,1)} %all-to-all-done.1, s32[16]{0:T(128)S(1)} %get-tuple-element.3), kind=kOutput, calls=%fused_computation.9 | convolution fusion | flops 68157952 | bytes 6291520 | tf_op jit(solution)/shard_map/go,ord->grd/dot_general | solution.py:51
  104.6 0.0 copy-start.1
  104.6 1.3 copy-done.1
  105.9 0.0 copy-done.3
  105.9 0.0 copy-start.7
  105.9 0.0 copy-start.5
  105.9 1.7 fusion.12
  107.6 1.1 pad_maximum_fusion
  108.7 0.0 all-reduce.2.cloned.1.call-update
  108.8 0.0 all-gather.2.cloned.1.call-start
  108.8 0.7 all-gather.2.cloned.1.call-update
  109.5 0.0 reduce-scatter.5.cloned.1.call-start
  109.6 0.1 iota_compare_fusion
  109.6 0.1 eq.76
  109.8 0.0 copy-done.7
  109.8 0.1 fusion.33
  109.8 75.4 %all-reduce.2.cloned.1.call-done = f32[16,128,128]{1,2,0:T(8,128)} async-done(((f32[16,128,128]{1,2,0:T(8,128)}), f32[16,128,128]{1,2,0:T(8,128)}) %all-reduce.2.cloned.1.call-update) | async-done | bytes 1048592 | tf_op jit(solution)/shard_map/psum | solution.py:73
  185.3 0.0 copy-done.5
  185.3 1.3 fusion.19
  186.6 0.0 copy-start.6
  186.6 0.9 convolution_multiply_fusion
  187.5 0.6 copy.70
  188.1 1.5 bitcast_select_fusion.1
  189.6 0.0 reduce-scatter.5.cloned.1.call-update
  189.7 0.3 reduce-scatter.3.cloned.1.call-start
  189.9 0.0 copy-done.6
  189.9 2.9 fusion.24
  192.8 6.1 %broadcast_multiply_fusion = f32[32,64,1024]{2,0,1:T(8,128)S(1)} fusion(f32[16,64,1024]{2,1,0:T(8,128)S(1)} %fusion.24, s32[16]{0:T(128)S(1)} %get-tuple-element.3), kind=kOutput, calls=%fused_computation.6 | convolution fusion | flops 404750848 | bytes 12582976 | tf_op jit(solution)/shard_map/go,grd->ord/dot_general | solution.py:101
  198.9 8.1 %copy.68 = f32[32,64,1024]{2,1,0:T(8,128)} copy(f32[32,64,1024]{2,0,1:T(8,128)S(1)} %broadcast_multiply_fusion) | data formatting | bytes 16777216 | tf_op jit(solution)/shard_map/mul | solution.py:101
  207.0 12.7 %bitcast_select_fusion = f32[64,64,1024]{2,1,0:T(8,128)} fusion(f32[32,64,1024]{2,1,0:T(8,128)} %copy.68, pred[64]{0:T(512)(128)(4,1)S(1)} %eq.76), kind=kLoop, calls=%fused_computation | loop fusion | flops 4194304 | bytes 25165888 | tf_op jit(solution)/shard_map/jit(_where)/select_n | solution.py:111
  219.7 0.0 reduce-scatter.3.cloned.1.call-update
  219.8 28.1 %all-gather.2.cloned.1.call-done = bf16[2048,1024]{1,0:T(8,128)(2,1)} async-done(((bf16[2048,128]{1,0:T(8,128)(2,1)}), bf16[2048,1024]{1,0:T(8,128)(2,1)}) %all-gather.2.cloned.1.call-update) | async-done | bytes 4194320 | tf_op jit(solution)/shard_map/all_gather | solution.py:77
  247.9 0.0 copy-done
  247.9 0.0 copy-start.2
  247.9 6.5 %fusion.42 = f32[2048,1024]{1,0:T(8,128)S(1)} fusion(bf16[2048,1024]{1,0:T(8,128)(2,1)} %all-gather.2.cloned.1.call-done, bf16[1024,1024]{1,0:T(8,128)(2,1)S(1)} %copy-done), kind=kOutput, calls=%fused_computation.53 | convolution fusion | flops 4294967296 | bytes 14680064 | tf_op jit(solution)/shard_map/dot_general | solution.py:76
  254.4 0.0 copy-done.2
  254.4 5.2 %multiply_convert_fusion = bf16[16,128,1024]{2,1,0:T(8,128)(2,1)} fusion(f32[16,128,1024]{2,1,0:T(8,128)S(1)} %bitcast.32, f32[16,128]{1,0:T(8,128)S(1)} %fusion.33, bf16[16,64,1024]{2,0,1:T(8,128)(2,1)S(1)} %copy-done.2, f32[16,128,128]{1,2,0:T(8,128)S(1)} %copy-done.6), kind=kOutput, calls=%fused_computation.1 | convolution fusion | flops 277086208 | bytes 15220736 | tf_op jit(solution)/shard_map/wks,wsx->wkx/dot_general | solution.py:82
  259.7 77.8 %reduce-scatter.5.cloned.1.call-done = f32[2,64,128]{2,1,0:T(8,128)} async-done(((f32[64,64,128]{2,1,0:T(8,128)}), f32[2,64,128]{2,1,0:T(8,128)}) %reduce-scatter.5.cloned.1.call-update) | async-done | bytes 65552 | tf_op jit(solution)/shard_map/reduce_scatter | solution.py:119
  337.5 127.2 %reduce-scatter.3.cloned.1.call-done = f32[2,64,1024]{2,1,0:T(8,128)} async-done(((f32[64,64,1024]{2,1,0:T(8,128)}), f32[2,64,1024]{2,1,0:T(8,128)}) %reduce-scatter.3.cloned.1.call-update) | async-done | bytes 524304 | tf_op jit(solution)/shard_map/reduce_scatter | solution.py:118
  (1 shorter events, 0.0 us)
Async XLA Ops:
  7.2 240.8 %copy-start = (bf16[1024,1024]{1,0:T(8,128)(2,1)S(1)}, bf16[1024,1024]{1,0:T(8,128)(2,1)}, u32[]{:S(2)}) copy-start(bf16[1024,1024]{1,0:T(8,128)(2,1)} %param.10) | copy-start | bytes 6291460
  24.8 15.5 %all-to-all-start.2 = ((bf16[32,64,128]{2,1,0:T(8,128)(2,1)}), bf16[32,64,128]{2,1,0:T(8,128)(2,1)S(1)}, u32[]{:S(2)}, u32[]{:S(2)}) async-start(bf16[32,64,128]{2,1,0:T(8,128)(2,1)} %copy.63), calls=%async_computation.2 | async-start | bytes 1048576 | tf_op jit(solution)/shard_map/all_to_all | solution.py:48
  36.4 10.4 %copy-start.4 = (bf16[2048,128]{1,0:T(8,128)(2,1)S(1)}, bf16[2048,128]{1,0:T(8,128)(2,1)}, u32[]{:S(2)}) copy-start(bf16[2048,128]{1,0:T(8,128)(2,1)} %param.9) | copy-start | bytes 1572868
  40.2 57.4 %all-to-all-start.1 = ((bf16[32,64,1024]{2,1,0:T(8,128)(2,1)}), bf16[32,64,1024]{2,1,0:T(8,128)(2,1)}, u32[]{:S(2)}, u32[]{:S(2)}) async-start(bf16[32,64,1024]{2,1,0:T(8,128)(2,1)} %copy.59), calls=%async_computation.1 | async-start | bytes 8388608 | tf_op jit(solution)/shard_map/all_to_all | solution.py:47
  46.2 139.1 %all-reduce.2.cloned.1.call-start = ((), (), s32[]{:S(2)}) async-start(), calls=%async_computation.6 | async-start | bytes 2097152 | tf_op jit(solution)/shard_map/psum | solution.py:73
  97.7 8.2 %copy-start.3 = (bf16[2048,1024]{1,0:T(8,128)(2,1)S(1)}, bf16[2048,1024]{1,0:T(8,128)(2,1)}, u32[]{:S(2)}) copy-start(bf16[2048,1024]{1,0:T(8,128)(2,1)} %param.8) | copy-start | bytes 12582916
  104.6 1.3 copy-start.1
  105.9 3.9 copy-start.7
  105.9 79.4 %copy-start.5 = (bf16[2048,128]{1,0:T(8,128)(2,1)S(1)}, bf16[2048,128]{1,0:T(8,128)(2,1)}, u32[]{:S(2)}) copy-start(bf16[2048,128]{1,0:T(8,128)(2,1)} %param.9) | copy-start | bytes 1572868
  108.8 139.1 %all-gather.2.cloned.1.call-start = ((), (), s32[]{:S(2)}) async-start(), calls=%async_computation.5 | async-start | bytes 4718592 | tf_op jit(solution)/shard_map/all_gather | solution.py:77
  109.5 228.0 %reduce-scatter.5.cloned.1.call-start = ((), (), s32[]{:S(2)}) async-start(), calls=%async_computation.8 | async-start | bytes 2162688 | tf_op jit(solution)/shard_map/reduce_scatter | solution.py:119
  186.6 3.4 copy-start.6
  189.7 275.1 %reduce-scatter.3.cloned.1.call-start = ((), (), s32[]{:S(2)}) async-start(), calls=%async_computation.7 | async-start | bytes 17301504 | tf_op jit(solution)/shard_map/reduce_scatter | solution.py:118
  247.9 6.5 %copy-start.2 = (bf16[16,64,1024]{2,0,1:T(8,128)(2,1)S(1)}, bf16[16,64,1024]{2,0,1:T(8,128)(2,1)}, u32[]{:S(2)}) copy-start(bf16[16,64,1024]{2,0,1:T(8,128)(2,1)} %copy-done.1) | copy-start | bytes 6291460
Sparse Core Ops, SparseCore 0:
  108.9 76.3 all-reduce.1
  187.0 60.8 all-gather.1
  252.3 85.1 reduce-scatter.4
  342.1 122.5 reduce-scatter.2
where the time goes:
time: 472 us; the launch traced here: 471 us
  waiting for transfers between devices  364 us (77%)
  matrix products  35.8 us (8%)
  other arithmetic  17.3 us (4%)
  local copies, waits for them, and re-layouts  15.6 us (3%)
  between operations  13.9 us (3%)
  blocking collectives  13.6 us (3%)
  starting transfers between devices  11.5 us (2%)
    reduce_scatter x1, waiting for transfers between devices, on_device(): lax.psum_scatter(dense_down, 'dp', scatter_dimension=0, tiled=True)  127 us
    reduce_scatter x1, waiting for transfers between devices, on_device(): lax.psum_scatter(dense_up, 'dp', scatter_dimension=0, tiled=True)  77.8 us
    psum x1, waiting for transfers between devices, on_device(): summed = lax.psum(partial_terms, 'tsp')  75.4 us
    all_to_all x1, waiting for transfers between devices, on_device(): lax.all_to_all(reply_down, 'dp', split_axis=0, concat_axis=0, tiled=True)  50.4 us
    all_gather x1, waiting for transfers between devices, on_device(): lax.all_gather(cotangent, 'tsp', axis=1, tiled=True)  28.1 us
    all_to_all x1, blocking collectives, on_device(): lax.all_to_all(wanted[:, None], 'dp', split_axis=0, concat_axis=0, tiled=...  13.6 us
    select_n x1, other arithmetic, on_device(): jnp.where(slot_match, slot_dgrad[:, None], 0.0)  12.7 us
  transfers between devices with their start and end apart: 6, of which 6 were waited for; matrix products, arithmetic and copies ran while one was open for 11% of the time, Pallas kernels for 0%

commit v1 on v0

--- a/solution.py
+++ b/solution.py
@@ -4,6 +4,16 @@
 from jax.sharding import PartitionSpec as P
 
 ADAPTER_SCALE = 2.0
+
+
+def inputs_bind(arr_in):
+    current_arr = jnp.concatenate(
+        jax.lax.all_to_all(
+            jnp.stack([arr_in for _ in range(jax.lax.axis_size("tsp"))]), "tsp", 0, 0
+        ),
+        1,
+    )
+    return current_arr
 
 
 def lookup(idents, mapping):
@@ -74,7 +84,7 @@
     reduced_rows = (summed[:, :, :rank_of_adapter] * live_rows[:, :, None]).astype(jnp.bfloat16)
     gathered_weights = (summed[:, :, rank_of_adapter:] * live_rows[:, :, None]).astype(jnp.bfloat16)
     frozen_output = lax.dot_general(
-        lax.all_gather(cotangent, "tsp", axis=1, tiled=True),
+        inputs_bind(cotangent),
         frozen_key_weight,
         (((1,), (1,)), ((), ())),
         preferred_element_type=jnp.float32,

time: 472 us -> 414 us (0.88)
  waiting for transfers between devices: 364 us -> 184 us
  blocking collectives: 13.6 us -> 109 us
  local copies, waits for them, and re-layouts: 15.6 us -> 36.6 us
    all_to_all x0 -> x1, blocking collectives: none -> 95.7 us  [inputs_bind(): jax.lax.all_to_all(jnp.stack([arr_in for _ in range(jax.lax.axis_size('ts...]
    reduce_scatter x1, waiting for transfers between devices: 77.8 us -> 0.01 us  [on_device(): lax.psum_scatter(dense_up, 'dp', scatter_dimension=0, tiled=True)]
    reduce_scatter x1, waiting for transfers between devices: 127 us -> 53.3 us  [on_device(): lax.psum_scatter(dense_down, 'dp', scatter_dimension=0, tiled=True)]
    all_gather x1 -> x0, waiting for transfers between devices: 28.1 us -> none  [on_device(): lax.all_gather(cotangent, 'tsp', axis=1, tiled=True)]
    reshape x0 -> x1, local copies, waits for them, and re-layouts: none -> 13.2 us  [inputs_bind(): jnp.concatenate(jax.lax.all_to_all(jnp.stack([arr_in for _ in range(jax.l...]
    dot_general x0 -> x1, local copies, waits for them, and re-layouts: none -> 7.28 us  [on_device(): lax.dot_general(inputs_bind(cotangent), frozen_key_weight, (((1,), (1,)),...]
  transfers between devices with their start and end apart: 6 -> 5, of which waited for: 6 -> 4; matrix products, arithmetic and copies ran while one was open for 11% -> 17% of each run, Pallas kernels for 0% -> 0%
where the time goes in v1:
time: 414 us; the launch traced here: 409 us
  waiting for transfers between devices  184 us (44%)
  blocking collectives  109 us (26%)
  local copies, waits for them, and re-layouts  36.6 us (9%)
  matrix products  36.2 us (9%)
  other arithmetic  17.3 us (4%)
  between operations  14.1 us (3%)
  starting transfers between devices  11.6 us (3%)
    all_to_all x1, blocking collectives, inputs_bind(): jax.lax.all_to_all(jnp.stack([arr_in for _ in range(jax.lax.axis_size('ts...  95.7 us
    psum x1, waiting for transfers between devices, on_device(): summed = lax.psum(partial_terms, 'tsp')  76.2 us
    reduce_scatter x1, waiting for transfers between devices, on_device(): lax.psum_scatter(dense_down, 'dp', scatter_dimension=0, tiled=True)  53.3 us
    all_to_all x1, waiting for transfers between devices, on_device(): lax.all_to_all(reply_down, 'dp', split_axis=0, concat_axis=0, tiled=True)  50.1 us
    all_to_all x1, blocking collectives, on_device(): lax.all_to_all(wanted[:, None], 'dp', split_axis=0, concat_axis=0, tiled=...  13.6 us
    reshape x1, local copies, waits for them, and re-layouts, inputs_bind(): jnp.concatenate(jax.lax.all_to_all(jnp.stack([arr_in for _ in range(jax.l...  13.2 us
    select_n x1, other arithmetic, on_device(): jnp.where(slot_match, slot_dgrad[:, None], 0.0)  12.8 us
  transfers between devices with their start and end apart: 5, of which 4 were waited for; matrix products, arithmetic and copies ran while one was open for 17% of the time, Pallas kernels for 0%

profile of v1, /device:TPU:2, one launch (start us, length us, event | category | flops | bytes accessed | tf_op | source)
XLA Modules:
  0.0 408.7 jit_solution(14124886071564476128)
XLA Ops:
  7.2 0.0 copy-start
  7.2 1.0 select_reduce_fusion.1
  8.2 0.1 select_reduce_fusion
  8.3 0.1 copy.61
  8.4 13.6 %all_to_all.24 = s32[32,1,1]{2,1,0:T(1,128)S(1)} all-to-all(s32[32,1,1]{2,1,0:T(1,128)S(1)} %copy.61), channel_id=1, replica_groups=mesh['dp'=32,'tsp'=8] {'dp'}, dimensions={0} | all-to-all | bytes 256 | tf_op jit(solution)/shard_map/all_to_all | solution.py:46
  22.0 0.7 reduce
  22.6 1.1 convolution_convert_fusion.1
  23.8 1.0 copy.67
  24.8 5.0 %all-to-all-start.3 = ((bf16[32,64,128]{2,1,0:T(8,128)(2,1)}), bf16[32,64,128]{2,1,0:T(8,128)(2,1)S(1)}, u32[]{:S(2)}, u32[]{:S(2)}) async-start(bf16[32,64,128]{2,1,0:T(8,128)(2,1)} %copy.67), calls=%async_computation.3 | async-start | bytes 1048576 | tf_op jit(solution)/shard_map/all_to_all | solution.py:58
  29.8 2.3 convolution_convert_fusion
  32.0 4.3 %copy.63 = bf16[32,64,1024]{2,1,0:T(8,128)(2,1)} copy(bf16[32,64,1024]{2,0,1:T(8,128)(2,1)S(1)} %convolution_convert_fusion) | data formatting | bytes 8388608 | tf_op jit(solution)/shard_map/convert_element_type | solution.py:52
  36.4 0.0 copy-start.4
  36.4 3.9 all-to-all-done.3
  40.2 5.9 %all-to-all-start.2 = ((bf16[32,64,1024]{2,1,0:T(8,128)(2,1)}), bf16[32,64,1024]{2,1,0:T(8,128)(2,1)}, u32[]{:S(2)}, u32[]{:S(2)}) async-start(bf16[32,64,1024]{2,1,0:T(8,128)(2,1)} %copy.63), calls=%async_computation.2 | async-start | bytes 8388608 | tf_op jit(solution)/shard_map/all_to_all | solution.py:57
  46.1 0.5 all-reduce.2.cloned.1.call-start
  46.7 0.4 convolution_convert_fusion.2
  47.1 0.0 copy-done.4
  47.1 0.5 convolution_bitcast_fusion
  47.5 50.1 %all-to-all-done.2 = bf16[32,64,1024]{2,1,0:T(8,128)(2,1)} async-done(((bf16[32,64,1024]{2,1,0:T(8,128)(2,1)}), bf16[32,64,1024]{2,1,0:T(8,128)(2,1)}, u32[]{:S(2)}, u32[]{:S(2)}) %all-to-all-start.2) | async-done | bytes 4194336 | tf_op jit(solution)/shard_map/all_to_all | solution.py:57
  97.7 0.0 copy-start.3
  97.7 6.9 %fusion.8 = bf16[16,64,1024]{2,0,1:T(8,128)(2,1)S(1)} fusion(bf16[32,64,1024]{2,1,0:T(8,128)(2,1)} %all-to-all-done.2, s32[16]{0:T(128)S(1)} %get-tuple-element.3), kind=kOutput, calls=%fused_computation.11 | convolution fusion | flops 68157952 | bytes 6291520 | tf_op jit(solution)/shard_map/go,ord->grd/dot_general | solution.py:61
  104.6 0.0 copy-start.1
  104.6 1.4 copy-done.1
  105.9 0.0 copy-done.3
  105.9 0.0 copy-start.6
  105.9 1.7 fusion.14
  107.7 1.1 pad_maximum_fusion
  108.7 0.0 all-reduce.2.cloned.1.call-update
  108.7 0.0 reduce-scatter.5.cloned.1.call-start
  108.8 0.1 iota_compare_fusion
  108.9 0.1 eq.76
  109.0 0.0 copy-done.6
  109.0 0.1 fusion.35
  109.1 76.2 %all-reduce.2.cloned.1.call-done = f32[16,128,128]{1,2,0:T(8,128)} async-done(((f32[16,128,128]{1,2,0:T(8,128)}), f32[16,128,128]{1,2,0:T(8,128)}) %all-reduce.2.cloned.1.call-update) | async-done | bytes 1048592 | tf_op jit(solution)/shard_map/psum | solution.py:83
  185.3 1.3 fusion.21
  186.6 0.9 convolution_multiply_fusion
  187.5 0.6 copy.74
  188.1 1.5 bitcast_select_fusion.1
  189.6 0.0 reduce-scatter.5.cloned.1.call-update
  189.6 0.2 reduce-scatter.3.cloned.1.call-start
  189.9 3.1 fusion.26
  192.9 6.1 %broadcast_multiply_fusion = f32[32,64,1024]{2,0,1:T(8,128)S(1)} fusion(f32[16,64,1024]{2,1,0:T(8,128)S(1)} %fusion.26, s32[16]{0:T(128)S(1)} %get-tuple-element.3), kind=kOutput, calls=%fused_computation.6 | convolution fusion | flops 404750848 | bytes 12582976 | tf_op jit(solution)/shard_map/go,grd->ord/dot_general | solution.py:111
  199.0 8.1 %copy.72 = f32[32,64,1024]{2,1,0:T(8,128)} copy(f32[32,64,1024]{2,0,1:T(8,128)S(1)} %broadcast_multiply_fusion) | data formatting | bytes 16777216 | tf_op jit(solution)/shard_map/mul | solution.py:111
  207.1 12.8 %bitcast_select_fusion = f32[64,64,1024]{2,1,0:T(8,128)} fusion(f32[32,64,1024]{2,1,0:T(8,128)} %copy.72, pred[64]{0:T(512)(128)(4,1)S(1)} %eq.76), kind=kLoop, calls=%fused_computation | loop fusion | flops 4194304 | bytes 25165888 | tf_op jit(solution)/shard_map/jit(_where)/select_n | solution.py:121
  219.9 0.0 reduce-scatter.3.cloned.1.call-update
  219.9 0.5 stack.2
  220.5 95.7 %all_to_all.25 = bf16[8,2048,128]{2,1,0:T(8,128)(2,1)S(1)} all-to-all(bf16[8,2048,128]{2,1,0:T(8,128)(2,1)S(1)} %stack.2), channel_id=1, replica_groups=mesh['dp'=32,'tsp'=8] {'tsp'}, dimensions={0} | all-to-all | bytes 8388608 | tf_op jit(solution)/shard_map/all_to_all | solution.py:11
  316.1 13.2 %copy.60 = bf16[2048,8,128]{2,1,0:T(8,128)(2,1)} copy(bf16[2048,8,128]{2,0,1:T(8,128)(2,1)S(1)} %bitcast.34) | data formatting | bytes 8388608 | tf_op jit(solution)/shard_map/reshape | solution.py:10
  329.3 7.3 %dot_general.42 = bf16[16,128,1024]{2,1,0:T(8,128)(2,1)} reshape(bf16[2048,8,128]{2,1,0:T(8,128)(2,1)} %copy.60) | data formatting | bytes 8388608 | tf_op jit(solution)/shard_map/dot_general | solution.py:86
  336.6 0.0 copy-done
  336.6 0.0 copy-start.2
  336.6 0.0 copy-start.5
  336.6 6.8 %fusion.6 = f32[16,128,1024]{2,1,0:T(8,128)S(1)} fusion(bf16[16,128,1024]{2,1,0:T(8,128)(2,1)} %dot_general.42, bf16[1024,1024]{1,0:T(8,128)(2,1)S(1)} %copy-done), kind=kOutput, calls=%fused_computation.9 | convolution fusion | flops 4294967296 | bytes 14680064 | tf_op jit(solution)/shard_map/dot_general | solution.py:86
  343.4 0.0 copy-done.2
  343.4 0.0 copy-done.5
  343.4 5.2 %multiply_convert_fusion = bf16[16,128,1024]{2,1,0:T(8,128)(2,1)} fusion(f32[16,128,1024]{2,1,0:T(8,128)S(1)} %fusion.6, f32[16,128]{1,0:T(8,128)S(1)} %fusion.35, bf16[16,64,1024]{2,0,1:T(8,128)(2,1)S(1)} %copy-done.2, f32[16,128,128]{1,2,0:T(8,128)S(1)} %copy-done.5), kind=kOutput, calls=%fused_computation.1 | convolution fusion | flops 277086208 | bytes 15220736 | tf_op jit(solution)/shard_map/wks,wsx->wkx/dot_general | solution.py:92
  348.6 0.0 reduce-scatter.5.cloned.1.call-done
  348.6 53.3 %reduce-scatter.3.cloned.1.call-done = f32[2,64,1024]{2,1,0:T(8,128)} async-done(((f32[64,64,1024]{2,1,0:T(8,128)}), f32[2,64,1024]{2,1,0:T(8,128)}) %reduce-scatter.3.cloned.1.call-update) | async-done | bytes 524304 | tf_op jit(solution)/shard_map/reduce_scatter | solution.py:128
  (1 shorter events, 0.0 us)
Async XLA Ops:
  7.2 329.4 %copy-start = (bf16[1024,1024]{1,0:T(8,128)(2,1)S(1)}, bf16[1024,1024]{1,0:T(8,128)(2,1)}, u32[]{:S(2)}) copy-start(bf16[1024,1024]{1,0:T(8,128)(2,1)} %param.10) | copy-start | bytes 6291460
  24.8 15.5 %all-to-all-start.3 = ((bf16[32,64,128]{2,1,0:T(8,128)(2,1)}), bf16[32,64,128]{2,1,0:T(8,128)(2,1)S(1)}, u32[]{:S(2)}, u32[]{:S(2)}) async-start(bf16[32,64,128]{2,1,0:T(8,128)(2,1)} %copy.67), calls=%async_computation.3 | async-start | bytes 1048576 | tf_op jit(solution)/shard_map/all_to_all | solution.py:58
  36.4 10.7 %copy-start.4 = (bf16[2048,128]{1,0:T(8,128)(2,1)S(1)}, bf16[2048,128]{1,0:T(8,128)(2,1)}, u32[]{:S(2)}) copy-start(bf16[2048,128]{1,0:T(8,128)(2,1)} %param.9) | copy-start | bytes 1572868
  40.2 57.4 %all-to-all-start.2 = ((bf16[32,64,1024]{2,1,0:T(8,128)(2,1)}), bf16[32,64,1024]{2,1,0:T(8,128)(2,1)}, u32[]{:S(2)}, u32[]{:S(2)}) async-start(bf16[32,64,1024]{2,1,0:T(8,128)(2,1)} %copy.63), calls=%async_computation.2 | async-start | bytes 8388608 | tf_op jit(solution)/shard_map/all_to_all | solution.py:57
  46.1 139.1 %all-reduce.2.cloned.1.call-start = ((), (), s32[]{:S(2)}) async-start(), calls=%async_computation.6 | async-start | bytes 2097152 | tf_op jit(solution)/shard_map/psum | solution.py:83
  97.7 8.3 %copy-start.3 = (bf16[2048,1024]{1,0:T(8,128)(2,1)S(1)}, bf16[2048,1024]{1,0:T(8,128)(2,1)}, u32[]{:S(2)}) copy-start(bf16[2048,1024]{1,0:T(8,128)(2,1)} %param.8) | copy-start | bytes 12582916
  104.6 1.4 copy-start.1
  105.9 3.1 copy-start.6
  108.7 239.9 %reduce-scatter.5.cloned.1.call-start = ((), (), s32[]{:S(2)}) async-start(), calls=%async_computation.8 | async-start | bytes 2162688 | tf_op jit(solution)/shard_map/reduce_scatter | solution.py:129
  189.6 212.3 %reduce-scatter.3.cloned.1.call-start = ((), (), s32[]{:S(2)}) async-start(), calls=%async_computation.7 | async-start | bytes 17301504 | tf_op jit(solution)/shard_map/reduce_scatter | solution.py:128
  336.6 6.8 %copy-start.2 = (bf16[16,64,1024]{2,0,1:T(8,128)(2,1)S(1)}, bf16[16,64,1024]{2,0,1:T(8,128)(2,1)}, u32[]{:S(2)}) copy-start(bf16[16,64,1024]{2,0,1:T(8,128)(2,1)} %copy-done.1) | copy-start | bytes 6291460
  336.6 6.8 %copy-start.5 = (f32[16,128,128]{1,2,0:T(8,128)S(1)}, f32[16,128,128]{1,2,0:T(8,128)}, u32[]{:S(2)}) copy-start(f32[16,128,128]{1,2,0:T(8,128)} %all-reduce.2.cloned.1.call-done) | copy-start | bytes 3145732
Sparse Core Ops, SparseCore 0:
  108.9 76.3 all-reduce.1
  189.8 84.7 reduce-scatter.4
  279.4 122.5 reduce-scatter.2
